TPU v7x, 256 devices: a whole 4x4x8 slice. The times are simulated.
256 devices in a mesh: rad: 8 (over x_hi, y), azi: 32 (over x_lo, z, core).
Axes of the slice: x: 4 (x_hi: 2, x_lo: 2; x = x_hi * 2 + x_lo), y: 4, z: 8, core: 2. Of those that a mesh axis runs over, the one named last changes fastest.
Arguments:
- tokens: bfloat16 [64, 512, 8, 512], P('rad', 'azi'), may hold values from -6 to 6
- cotangent: bfloat16 [64, 512, 8, 512], P('rad', 'azi'), may hold values from -6 to 6
- ln_gain: float32 [512], replicated, may hold values from 0.5 to 1.5
- qkv_weight: bfloat16 [512, 1536], P('azi'), may hold values from -2 to 2
- out_weight: bfloat16 [512, 512], P('azi'), may hold values from -0.25 to 0.25
- shear_offset: int32 [1], replicated, may hold values from 0 to 511
- window_shift: int32 [3], replicated, may hold values from 1 to 7, as said below
Outputs:
- block_out: bfloat16 [64, 512, 8, 512], P('rad', 'azi')
- grad_tokens: bfloat16 [64, 512, 8, 512], P('rad', 'azi')
- grad_qkv: float32 [512, 1536], P('azi')
- grad_out: float32 [512, 512], P('azi')
- grad_gain: float32 [512], replicated
Inputs may be any that keep to these rules, and one draw needn't show every extreme that they name: `window_shift`: the radial entry lies in 1 to 3; the azimuthal and vertical entries lie in 1 to 7, and one of these two equals 7.
All inputs are finite; a program needn't handle non-finite values.
Results may differ from a plain program's by a relative error of at most 0.025.
Values may be sent and summed in bfloat16 or wider, within the bound.
A program may use at most 192 MiB of HBM per device.

v0:
```python
import jax
import jax.numpy as jnp
from jax import lax
from jax.sharding import PartitionSpec as P

HEADS = 16
HD = 32
WR = 4
WA = 8
WZ = 8
EPS = 1e-05


def shifted_2(block, axis, distance):
    devices = range(lax.axis_size(axis))
    route = [((i - distance) % len(devices), i) for i in devices]
    return lax.ppermute(block, axis, route)


def to_windows(tensor, parts):
    extent_r, extent_a, extent_z, channels = tensor.shape
    tensor = tensor.reshape(
        extent_r // WR, WR, extent_a // WA, WA, extent_z // WZ, WZ, parts, HEADS, HD
    )
    tensor = tensor.transpose(0, 2, 4, 6, 7, 1, 3, 5, 8)
    return tensor.reshape(-1, parts, HEADS, WR * WA * WZ, HD)


def from_windows(windows, extent_r, extent_a, extent_z):
    parts = windows.shape[1]
    windows = windows.reshape(
        extent_r // WR, extent_a // WA, extent_z // WZ, parts, HEADS, WR, WA, WZ, HD
    )
    windows = windows.transpose(0, 5, 1, 6, 2, 7, 3, 4, 8)
    return windows.reshape(extent_r, extent_a, extent_z, parts * HEADS * HD)


def azi_roll(pieces, amount):
    cols_dev = pieces[0].shape[1]
    device_hops = amount // cols_dev
    remainder = amount % cols_dev
    current = pieces
    bit_count = (lax.axis_size("azi") - 1).bit_length()
    for bit_level in range(bit_count):
        hopped = shifted_2((current[0], current[1]), "azi", -(1 << bit_level))
        chosen = device_hops >> bit_level & 1 == 1
        current = (
            jnp.where(chosen, hopped[0], current[0]),
            jnp.where(chosen, hopped[1], current[1]),
        )
    following = shifted_2((current[0], current[1]), "azi", -1)
    return tuple(
        (
            lax.dynamic_slice_in_dim(
                jnp.concatenate([mine, theirs], axis=1), remainder, cols_dev, 1
            )
            for mine, theirs in zip(current, following)
        )
    )


def vertical_roll(field, start):
    depth = field.shape[2]
    return lax.dynamic_slice_in_dim(jnp.concatenate([field, field], axis=2), start, depth, 2)


def shift_in(first, second, shift_rad, shift_azi, shift_ver, offset, total_cols):
    rim_rows = WR - 1
    rows_dev, cols_dev, depth, width = first.shape
    below = shifted_2((first[:rim_rows], second[:rim_rows]), "rad", -1)
    extended = (
        jnp.concatenate([first, below[0]], axis=0),
        jnp.concatenate([second, below[1]], axis=0),
    )
    leading = shifted_2((extended[0][:, : WA - 1], extended[1][:, : WA - 1]), "azi", -1)
    rolled = tuple(
        (
            lax.dynamic_slice_in_dim(
                jnp.concatenate([own_part, lead_part], axis=1), shift_azi, cols_dev, 1
            )
            for own_part, lead_part in zip(extended, leading)
        )
    )
    wrapped = azi_roll(below, (offset + shift_azi) % total_cols)
    last_row = lax.axis_index("rad") == lax.axis_size("rad") - 1
    results = []
    for rolled_part, wrapped_part in zip(rolled, wrapped):
        joined = jnp.concatenate(
            [rolled_part[:rows_dev], jnp.where(last_row, wrapped_part, rolled_part[rows_dev:])],
            axis=0,
        )
        joined = lax.dynamic_slice_in_dim(joined, shift_rad, rows_dev, 0)
        results.append(vertical_roll(joined, shift_ver))
    return (results[0], results[1])


def shift_out(first, second, shift_rad, shift_azi, shift_ver, offset, total_cols):
    rim_rows = WR - 1
    rows_dev, cols_dev, depth, width = first.shape
    above = shifted_2((first[rows_dev - rim_rows :], second[rows_dev - rim_rows :]), "rad", 1)
    extended = (
        jnp.concatenate([above[0], first], axis=0),
        jnp.concatenate([above[1], second], axis=0),
    )
    trailing = shifted_2(
        (extended[0][:, cols_dev - (WA - 1) :], extended[1][:, cols_dev - (WA - 1) :]), "azi", 1
    )
    rolled = tuple(
        (
            lax.dynamic_slice_in_dim(
                jnp.concatenate([trail_part, own_part], axis=1), WA - 1 - shift_azi, cols_dev, 1
            )
            for own_part, trail_part in zip(extended, trailing)
        )
    )
    amount = (total_cols - (offset + shift_azi) % total_cols) % total_cols
    wrapped = azi_roll(above, amount)
    first_row = lax.axis_index("rad") == 0
    results = []
    for rolled_part, wrapped_part in zip(rolled, wrapped):
        joined = jnp.concatenate(
            [jnp.where(first_row, wrapped_part, rolled_part[:rim_rows]), rolled_part[rim_rows:]],
            axis=0,
        )
        joined = lax.dynamic_slice_in_dim(joined, rim_rows - shift_rad, rows_dev, 0)
        results.append(vertical_roll(joined, depth - shift_ver))
    return (results[0], results[1])


def on_device(tokens, cotangent, ln_gain, qkv_weight, out_weight, shear_offset, window_shift):
    rows_dev, cols_dev, depth, width = tokens.shape
    number = rows_dev * cols_dev * depth
    n_rad = lax.axis_size("rad")
    n_azi = lax.axis_size("azi")
    total_cols = cols_dev * n_azi
    shift_rad = window_shift[0]
    shift_azi = window_shift[1]
    shift_ver = window_shift[2]
    offset = shear_offset[0]
    contract = (((0,), (0,)), ((), ()))
    scaling = HD ** (-0.5)
    shifted, grad_in = shift_in(
        tokens, cotangent, shift_rad, shift_azi, shift_ver, offset, total_cols
    )
    inputs_f = shifted.astype(jnp.float32).reshape(number, width)
    centre = jnp.mean(inputs_f, axis=1, keepdims=True)
    centred = inputs_f - centre
    variance = jnp.mean(centred * centred, axis=1, keepdims=True)
    inverse_std = lax.rsqrt(variance + EPS)
    normed = centred * inverse_std
    hidden = (normed * ln_gain).astype(jnp.bfloat16)
    qkv_full, out_full = (
        lax.all_gather(qkv_weight, "azi", axis=0, tiled=True),
        lax.all_gather(out_weight, "azi", axis=0, tiled=True),
    )
    qkv = jnp.dot(hidden, qkv_full, preferred_element_type=jnp.float32)
    qkv = qkv.astype(jnp.bfloat16)
    windows = to_windows(qkv.reshape(rows_dev, cols_dev, depth, 3 * width), 3)
    queries, keys_win, values = (windows[:, 0], windows[:, 1], windows[:, 2])
    scores = (
        jnp.einsum("nhqd,nhkd->nhqk", queries, keys_win, preferred_element_type=jnp.float32)
        * scaling
    )
    weights = jax.nn.softmax(scores, axis=-1)
    weights_low = weights.astype(jnp.bfloat16)
    mixed = jnp.einsum(
        "nhqk,nhkd->nhqd", weights_low, values, preferred_element_type=jnp.float32
    ).astype(jnp.bfloat16)
    attended = from_windows(mixed[:, None], rows_dev, cols_dev, depth).reshape(number, width)
    branch = jnp.dot(attended, out_full, preferred_element_type=jnp.float32)
    out_shifted = (inputs_f + branch).astype(jnp.bfloat16)
    grad_low = grad_in.reshape(number, width)
    d_attended = jnp.dot(grad_low, out_full.T, preferred_element_type=jnp.float32)
    d_attended = d_attended.astype(jnp.bfloat16)
    d_windows = to_windows(d_attended.reshape(rows_dev, cols_dev, depth, width), 1)[:, 0]
    d_weights = jnp.einsum("nhqd,nhkd->nhqk", d_windows, values, preferred_element_type=jnp.float32)
    d_values = jnp.einsum(
        "nhqk,nhqd->nhkd", weights_low, d_windows, preferred_element_type=jnp.float32
    )
    d_scores = (
        weights * (d_weights - jnp.sum(weights * d_weights, axis=-1, keepdims=True))
    ).astype(jnp.bfloat16)
    d_queries = (
        jnp.einsum("nhqk,nhkd->nhqd", d_scores, keys_win, preferred_element_type=jnp.float32)
        * scaling
    )
    d_keys = (
        jnp.einsum("nhqk,nhqd->nhkd", d_scores, queries, preferred_element_type=jnp.float32)
        * scaling
    )
    d_stack = jnp.stack([d_queries, d_keys, d_values], axis=1).astype(jnp.bfloat16)
    d_qkv = from_windows(d_stack, rows_dev, cols_dev, depth).reshape(number, 3 * width)
    d_hidden = jnp.dot(d_qkv, qkv_full.T, preferred_element_type=jnp.float32)
    d_normed = d_hidden * ln_gain
    d_branch = inverse_std * (
        d_normed
        - jnp.mean(d_normed, axis=1, keepdims=True)
        - normed * jnp.mean(d_normed * normed, axis=1, keepdims=True)
    )
    grad_shifted = (grad_low.astype(jnp.float32) + d_branch).astype(jnp.bfloat16)
    shape_out = (rows_dev, cols_dev, depth, width)
    block_out, grad_tokens = shift_out(
        out_shifted.reshape(shape_out),
        grad_shifted.reshape(shape_out),
        shift_rad,
        shift_azi,
        shift_ver,
        offset,
        total_cols,
    )
    term_qkv = lax.dot_general(hidden, d_qkv, contract, preferred_element_type=jnp.float32)
    term_out = lax.dot_general(attended, grad_low, contract, preferred_element_type=jnp.float32)
    whole_term = lax.psum(jnp.concatenate([term_qkv, term_out], axis=1).astype(jnp.bfloat16), "rad")
    share = lax.psum_scatter(whole_term, "azi", scatter_dimension=0, tiled=True).astype(jnp.float32)
    gain_total = lax.psum(jnp.sum(d_hidden * normed, axis=0), ("rad", "azi"))
    factor = float(number * n_rad * n_azi) ** (-0.5)
    grad_qkv = share[:, : 3 * width] * factor
    grad_out = share[:, 3 * width :] * factor
    return (block_out, grad_tokens, grad_qkv, grad_out, gain_total * factor)


def solution(mesh):
    in_specs = (
        P("rad", "azi", None, None),
        P("rad", "azi", None, None),
        P(),
        P("azi", None),
        P("azi", None),
        P(),
        P(),
    )
    out_specs = (
        P("rad", "azi", None, None),
        P("rad", "azi", None, None),
        P("azi", None),
        P("azi", None),
        P(),
    )
    return jax.shard_map(
        on_device, mesh=mesh, in_specs=in_specs, out_specs=out_specs, check_vma=False
    )
```

profile of v0, /device:TPU:32, one launch (start us, length us, event | category | flops | bytes accessed | tf_op | source)
XLA Modules:
  0.0 756.4 jit_solution(11868625129123604809)
XLA Ops:
  49.3 9.5 %collective-permute-start.20 = (bf16[3,16,8,512]{3,2,1,0:T(8,128)(2,1)}, bf16[3,16,8,512]{3,2,1,0:T(8,128)(2,1)}, u32[]{:S(2)}, u32[]{:S(2)}) collective-permute-start(bf16[3,16,8,512]{3,2,1,0:T(8,128)(2,1)} %broadcast_select_fusion.2), channel_id=1, source_target_pairs={{4,0},{5,1},{6,2},{7,3},{8,4},{9,5},{10,6},{11,7},{12,8},{13,9},{1... | collective-permute-start | bytes 1179656 | tf_op jit(solution)/shard_map/ppermute | solution.py:17
  60.8 10.2 %collective-permute-start.4 = (bf16[3,16,8,512]{3,2,1,0:T(8,128)(2,1)S(1)}, bf16[3,16,8,512]{3,2,1,0:T(8,128)(2,1)}, u32[]{:S(2)}, u32[]{:S(2)}) collective-permute-start(bf16[3,16,8,512]{3,2,1,0:T(8,128)(2,1)S(1)} %broadcast_select_fusion.3), channel_id=1, source_target_pairs={{4,0},{5,1},{6,2},{7,3},{8,4},{9,5},{10,6},{11,7},{12,8},{13,9},{1... | collective-permute-start | bytes 1179656 | tf_op jit(solution)/shard_map/ppermute | solution.py:17
  84.4 70.5 %all_gather.7 = bf16[512,512]{1,0:T(8,128)(2,1)} all-gather(bf16[16,512]{1,0:T(8,128)(2,1)S(1)} %copy-done.14), channel_id=1, replica_groups=mesh['rad'=8,'azi'=32] {'azi'}, dimensions={0}, use_global_device_ids=true | all-gather | bytes 540672 | tf_op jit(solution)/shard_map/all_gather | solution.py:154
  166.9 19.8 %collective-permute-done.5 = bf16[3,16,8,512]{3,2,1,0:T(8,128)(2,1)S(1)} collective-permute-done((bf16[3,16,8,512]{3,2,1,0:T(8,128)(2,1)S(1)}, bf16[3,16,8,512]{3,2,1,0:T(8,128)(2,1)S(1)}, u32[]{:S(2)}, u32[]{:S(2)}) %collective-permute-start.5) | collective-permute-done | bytes 393248 | tf_op jit(solution)/shard_map/ppermute | solution.py:17
  186.8 10.8 %collective-permute-start.6 = (bf16[3,16,8,512]{3,2,1,0:T(8,128)(2,1)S(1)}, bf16[3,16,8,512]{3,2,1,0:T(8,128)(2,1)S(1)}, u32[]{:S(2)}, u32[]{:S(2)}) collective-permute-start(bf16[3,16,8,512]{3,2,1,0:T(8,128)(2,1)S(1)} %broadcast_select_fusion.7), channel_id=1, source_target_pairs={{16,0},{17,1},{18,2},{19,3},{20,4},{21,5},{22,6},{23,7},{24,8},{25... | collective-permute-start | bytes 1179656 | tf_op jit(solution)/shard_map/ppermute | solution.py:17
  230.1 14.6 %reshape_reshape.12 = bf16[2,4,2,8,1,8,3,16,32]{8,7,6,5,3,2,1,0,4:T(8,128)(2,1)} reshape(bf16[1024,1536]{1,0:T(8,128)(2,1)} %convolution_convert_fusion) | data formatting | bytes 6291456 | tf_op jit(solution)/shard_map/reshape;reshape | solution.py:22
  244.6 12.8 %copy.19 = bf16[2,4,2,8,1,8,3,16,32]{8,5,3,1,7,6,2,0,4:T(8,128)(2,1)} copy(bf16[2,4,2,8,1,8,3,16,32]{8,7,6,5,3,2,1,0,4:T(8,128)(2,1)} %reshape_reshape.12) | data formatting | bytes 6291456 | tf_op jit(solution)/shard_map/reshape;reshape | solution.py:22
  257.4 11.6 %fusion.11 = f32[4,16,256,256]{2,3,1,0:T(8,128)} fusion(bf16[4,3,16,256,32]{4,3,2,1,0:T(8,128)(2,1)} %bitcast.105), kind=kOutput, calls=%fused_computation.19 | convolution fusion | flops 268435456 | bytes 25165824 | tf_op jit(solution)/shard_map/nhqd,nhkd->nhqk/dot_general | solution.py:161
  269.0 19.6 %fusion.62 = (f32[4,16,256]{2,1,0:T(8,128)S(1)}, f32[4,16,256,256]{2,3,1,0:T(8,128)}) fusion(f32[4,16,256,256]{2,3,1,0:T(8,128)} %fusion.11), kind=kOutput, calls=%fused_computation.143 | output fusion | flops 16777472 | bytes 33619968 | tf_op jit(solution)/shard_map/sub | solution.py:164
  288.6 14.5 %multiply_reduce_fusion = (f32[4,16,256]{2,1,0:T(8,128)S(1)}, f32[4,16,256,256]{2,3,1,0:T(8,128)}) fusion(f32[4,16,256,256]{2,3,1,0:T(8,128)} %get-tuple-element.18, f32[4,16,256]{2,1,0:T(8,128)S(1)} %get-tuple-element.17, bf16[4,16,256,32]{3,2,1,0:T(8,128)(2,1)} %bitcast.120, bf16[4,3,16,256,32]{4,3,2,1,0:T(8,128)(2,1)} %bitcast.106), kind=kOutput, calls=%fused_computation.2 | convolution fusion | flops 281001984 | bytes 42074112 | tf_op jit(solution)/shard_map/nhqd,nhkd->nhqk/dot_general | solution.py:176
  303.1 11.7 %multiply_convert_fusion = bf16[4,16,256,256]{2,3,1,0:T(8,128)(2,1)S(1)} fusion(f32[4,16,256,256]{2,3,1,0:T(8,128)} %get-tuple-element.20, f32[4,16,256]{2,1,0:T(8,128)S(1)} %get-tuple-element.19, f32[4,16,256,256]{2,3,1,0:T(8,128)} %get-tuple-element.18, f32[4,16,256]{2,1,0:T(8,128)S(1)} %get-tuple-element.17), kind=kLoop, calls=%fused_computation.1 | loop fusion | flops 16777216 | bytes 42074112 | tf_op jit(solution)/shard_map/convert_element_type | solution.py:182
  328.9 9.3 %fusion.34 = bf16[4,16,256,32]{2,3,1,0:T(8,128)(2,1)} fusion(bf16[4,16,256,32]{3,2,1,0:T(8,128)(2,1)} %bitcast.121, f32[4,16,256,256]{2,3,1,0:T(8,128)} %get-tuple-element.18, f32[4,16,256]{2,1,0:T(8,128)S(1)} %get-tuple-element.17), kind=kOutput, calls=%fused_computation.67 | convolution fusion | flops 277348352 | bytes 18939904 | tf_op jit(solution)/shard_map/nhqk,nhqd->nhkd/dot_general | solution.py:177
  338.1 9.7 %fusion.31 = bf16[4,16,256,32]{2,3,1,0:T(8,128)(2,1)} fusion(bf16[4,3,16,256,32]{4,3,2,1,0:T(8,128)(2,1)} %bitcast.109, f32[4,16,256,256]{2,3,1,0:T(8,128)} %get-tuple-element.18, f32[4,16,256]{2,1,0:T(8,128)S(1)} %get-tuple-element.17), kind=kOutput, calls=%fused_computation.66 | convolution fusion | flops 277348352 | bytes 22085632 | tf_op jit(solution)/shard_map/nhqk,nhkd->nhqd/dot_general | solution.py:166
  363.2 16.4 %copy.35 = bf16[2,4,2,8,1,8,3,16,32]{8,7,6,5,3,2,1,0,4:T(8,128)(2,1)} copy(bf16[2,4,2,8,1,8,3,16,32]{8,5,3,1,7,2,0,6,4:T(8,128)(2,1)S(1)} %maximum_bitcast_fusion) | data formatting | bytes 6291456 | tf_op jit(solution)/shard_map/transpose | solution.py:34
  379.7 17.1 %reshape_reshape.15 = bf16[1024,1536]{1,0:T(8,128)(2,1)} reshape(bf16[2,4,2,8,1,8,3,16,32]{8,7,6,5,3,2,1,0,4:T(8,128)(2,1)} %copy.35) | data formatting | bytes 6291456 | tf_op jit(solution)/shard_map/reshape;reshape | solution.py:192
  399.8 10.8 %copy.25 = bf16[2,4,2,8,1,8,1,16,32]{8,7,5,3,2,1,0,6,4:T(8,128)(2,1)} copy(bf16[2,4,2,8,1,8,1,16,32]{8,5,3,1,7,2,0,6,4:T(8,128)(2,1)} %bitcast.110) | data formatting | bytes 2097152 | tf_op jit(solution)/shard_map/transpose | solution.py:34
  427.3 12.5 %collective-permute-done.24 = bf16[3,16,8,512]{3,2,1,0:T(8,128)(2,1)S(1)} collective-permute-done((bf16[3,16,8,512]{3,2,1,0:T(8,128)(2,1)S(1)}, bf16[3,16,8,512]{3,2,1,0:T(8,128)(2,1)S(1)}, u32[]{:S(2)}, u32[]{:S(2)}) %collective-permute-start.24) | collective-permute-done | bytes 393248 | tf_op jit(solution)/shard_map/ppermute | solution.py:17
  448.0 10.6 %collective-permute-start.26 = (bf16[3,16,8,512]{3,2,1,0:T(8,128)(2,1)S(1)}, bf16[3,16,8,512]{3,2,1,0:T(8,128)(2,1)}, u32[]{:S(2)}, u32[]{:S(2)}) collective-permute-start(bf16[3,16,8,512]{3,2,1,0:T(8,128)(2,1)S(1)} %broadcast_select_fusion.10), channel_id=1, source_target_pairs={{2,0},{3,1},{4,2},{5,3},{6,4},{7,5},{8,6},{9,7},{10,8},{11,9},{12,... | collective-permute-start | bytes 1179656 | tf_op jit(solution)/shard_map/ppermute | solution.py:17
  462.6 77.5 %psum.15 = f32[512]{0:T(512)S(1)} all-reduce(f32[512]{0:T(512)S(1)} %get-tuple-element.5), channel_id=1, replica_groups=mesh['rad'=8,'azi'=32] {'rad','azi'}, use_global_device_ids=true, to_apply=%region_10.11 | all-reduce | flops 512 | bytes 4096 | tf_op jit(solution)/shard_map/psum | solution.py:215
  543.3 18.2 %collective-permute-done.10 = bf16[3,16,8,512]{3,2,1,0:T(8,128)(2,1)S(1)} collective-permute-done((bf16[3,16,8,512]{3,2,1,0:T(8,128)(2,1)S(1)}, bf16[3,16,8,512]{3,2,1,0:T(8,128)(2,1)S(1)}, u32[]{:S(2)}, u32[]{:S(2)}) %collective-permute-start.10) | collective-permute-done | bytes 393248 | tf_op jit(solution)/shard_map/ppermute | solution.py:17
  571.4 30.7 %collective-permute-start.15 = (bf16[11,7,8,512]{3,2,1,0:T(8,128)(2,1)S(1)}, bf16[11,7,8,512]{3,2,1,0:T(8,128)(2,1)S(1)}, u32[]{:S(2)}, u32[]{:S(2)}) collective-permute-start(bf16[11,7,8,512]{3,2,1,0:T(8,128)(2,1)S(1)} %pad_maximum_fusion.2), channel_id=1, source_target_pairs={{31,0},{0,1},{1,2},{2,3},{3,4},{4,5},{5,6},{6,7},{7,8},{8,9},{9,10... | collective-permute-start | bytes 1892360 | tf_op jit(solution)/shard_map/ppermute | solution.py:17
  604.7 22.3 %collective-permute-done.31 = bf16[11,7,8,512]{3,2,1,0:T(8,128)(2,1)S(1)} collective-permute-done((bf16[11,7,8,512]{3,2,1,0:T(8,128)(2,1)S(1)}, bf16[11,7,8,512]{3,2,1,0:T(8,128)(2,1)S(1)}, u32[]{:S(2)}, u32[]{:S(2)}) %collective-permute-start.31) | collective-permute-done | bytes 630816 | tf_op jit(solution)/shard_map/ppermute | solution.py:17
  631.1 16.9 %collective-permute-start.30 = (bf16[3,16,8,512]{3,2,1,0:T(8,128)(2,1)S(1)}, bf16[3,16,8,512]{3,2,1,0:T(8,128)(2,1)S(1)}, u32[]{:S(2)}, u32[]{:S(2)}) collective-permute-start(bf16[3,16,8,512]{3,2,1,0:T(8,128)(2,1)S(1)} %broadcast_select_fusion.18), channel_id=1, source_target_pairs={{1,0},{2,1},{3,2},{4,3},{5,4},{6,5},{7,6},{8,7},{9,8},{10,9},{11,1... | collective-permute-start | bytes 1179656 | tf_op jit(solution)/shard_map/ppermute | solution.py:17
  662.0 85.3 %all-reduce.2.cloned.1.call-done = bf16[16,2048]{1,0:T(8,128)(2,1)} async-done(((bf16[16,2048]{1,0:T(8,128)(2,1)}), bf16[16,2048]{1,0:T(8,128)(2,1)}) %all-reduce.2.cloned.1.call-update) | async-done | bytes 65552 | tf_op jit(solution)/shard_map/psum | solution.py:213
  (175 shorter events, 187.8 us)
Async XLA Ops:
  7.2 218.0 %all-gather.2.cloned.1.call-start = ((), (), s32[]{:S(2)}) async-start(), calls=%async_computation.1 | async-start | bytes 1622016 | tf_op jit(solution)/shard_map/all_gather | solution.py:153
  49.3 29.0 %collective-permute-start.20 = (bf16[3,16,8,512]{3,2,1,0:T(8,128)(2,1)}, bf16[3,16,8,512]{3,2,1,0:T(8,128)(2,1)}, u32[]{:S(2)}, u32[]{:S(2)}) collective-permute-start(bf16[3,16,8,512]{3,2,1,0:T(8,128)(2,1)} %broadcast_select_fusion.2), channel_id=1, source_target_pairs={{4,0},{5,1},{6,2},{7,3},{8,4},{9,5},{10,6},{11,7},{12,8},{13,9},{1... | collective-permute-start | bytes 1179656 | tf_op jit(solution)/shard_map/ppermute | solution.py:17
  58.8 601.5 %reduce-scatter.2.cloned.1.call-start = ((), (), s32[]{:S(2)}) async-start(), calls=%async_computation.2 | async-start | bytes 2162688 | tf_op jit(solution)/shard_map/reduce_scatter | solution.py:214
  59.8 105.6 %collective-permute-start.17 = (bf16[11,7,8,512]{3,2,1,0:T(8,128)(2,1)}, bf16[11,7,8,512]{3,2,1,0:T(8,128)(2,1)}, u32[]{:S(2)}, u32[]{:S(2)}) collective-permute-start(bf16[11,7,8,512]{3,2,1,0:T(8,128)(2,1)} %slice.113), channel_id=1, source_target_pairs={{1,0},{2,1},{3,2},{4,3},{5,4},{6,5},{7,6},{8,7},{9,8},{10,9},{11,1... | collective-permute-start | bytes 1892360 | tf_op jit(solution)/shard_map/ppermute | solution.py:17
  60.8 100.2 %collective-permute-start.4 = (bf16[3,16,8,512]{3,2,1,0:T(8,128)(2,1)S(1)}, bf16[3,16,8,512]{3,2,1,0:T(8,128)(2,1)}, u32[]{:S(2)}, u32[]{:S(2)}) collective-permute-start(bf16[3,16,8,512]{3,2,1,0:T(8,128)(2,1)S(1)} %broadcast_select_fusion.3), channel_id=1, source_target_pairs={{4,0},{5,1},{6,2},{7,3},{8,4},{9,5},{10,6},{11,7},{12,8},{13,9},{1... | collective-permute-start | bytes 1179656 | tf_op jit(solution)/shard_map/ppermute | solution.py:17
  80.1 82.6 %collective-permute-start.21 = (bf16[3,16,8,512]{3,2,1,0:T(8,128)(2,1)}, bf16[3,16,8,512]{3,2,1,0:T(8,128)(2,1)}, u32[]{:S(2)}, u32[]{:S(2)}) collective-permute-start(bf16[3,16,8,512]{3,2,1,0:T(8,128)(2,1)} %broadcast_select_fusion.4), channel_id=1, source_target_pairs={{8,0},{9,1},{10,2},{11,3},{12,4},{13,5},{14,6},{15,7},{16,8},{17,9... | collective-permute-start | bytes 1179656 | tf_op jit(solution)/shard_map/ppermute | solution.py:17
  160.9 36.9 %collective-permute-start.1 = (bf16[11,7,8,512]{3,2,1,0:T(8,128)(2,1)S(1)}, bf16[11,7,8,512]{3,2,1,0:T(8,128)(2,1)S(1)}, u32[]{:S(2)}, u32[]{:S(2)}) collective-permute-start(bf16[11,7,8,512]{3,2,1,0:T(8,128)(2,1)S(1)} %slice.104), channel_id=1, source_target_pairs={{1,0},{2,1},{3,2},{4,3},{5,4},{6,5},{7,6},{8,7},{9,8},{10,9},{11,1... | collective-permute-start | bytes 1892360 | tf_op jit(solution)/shard_map/ppermute | solution.py:17
  162.0 24.8 %collective-permute-start.5 = (bf16[3,16,8,512]{3,2,1,0:T(8,128)(2,1)S(1)}, bf16[3,16,8,512]{3,2,1,0:T(8,128)(2,1)S(1)}, u32[]{:S(2)}, u32[]{:S(2)}) collective-permute-start(bf16[3,16,8,512]{3,2,1,0:T(8,128)(2,1)S(1)} %broadcast_select_fusion.5), channel_id=1, source_target_pairs={{8,0},{9,1},{10,2},{11,3},{12,4},{13,5},{14,6},{15,7},{16,8},{17,9... | collective-permute-start | bytes 1179656 | tf_op jit(solution)/shard_map/ppermute | solution.py:17
  163.7 33.9 %collective-permute-start.22 = (bf16[3,16,8,512]{3,2,1,0:T(8,128)(2,1)S(1)}, bf16[3,16,8,512]{3,2,1,0:T(8,128)(2,1)S(1)}, u32[]{:S(2)}, u32[]{:S(2)}) collective-permute-start(bf16[3,16,8,512]{3,2,1,0:T(8,128)(2,1)S(1)} %broadcast_select_fusion.6), channel_id=1, source_target_pairs={{16,0},{17,1},{18,2},{19,3},{20,4},{21,5},{22,6},{23,7},{24,8},{25... | collective-permute-start | bytes 1179656 | tf_op jit(solution)/shard_map/ppermute | solution.py:17
  186.8 19.1 %collective-permute-start.6 = (bf16[3,16,8,512]{3,2,1,0:T(8,128)(2,1)S(1)}, bf16[3,16,8,512]{3,2,1,0:T(8,128)(2,1)S(1)}, u32[]{:S(2)}, u32[]{:S(2)}) collective-permute-start(bf16[3,16,8,512]{3,2,1,0:T(8,128)(2,1)S(1)} %broadcast_select_fusion.7), channel_id=1, source_target_pairs={{16,0},{17,1},{18,2},{19,3},{20,4},{21,5},{22,6},{23,7},{24,8},{25... | collective-permute-start | bytes 1179656 | tf_op jit(solution)/shard_map/ppermute | solution.py:17
  424.8 23.2 %collective-permute-start.8 = (bf16[3,16,8,512]{3,2,1,0:T(8,128)(2,1)}, bf16[3,16,8,512]{3,2,1,0:T(8,128)(2,1)S(1)}, u32[]{:S(2)}, u32[]{:S(2)}) collective-permute-start(bf16[3,16,8,512]{3,2,1,0:T(8,128)(2,1)} %bitcast.13), channel_id=1, source_target_pairs={{224,0},{0,32},{32,64},{64,96},{96,128},{128,160},{160,192},{192,2... | collective-permute-start | bytes 1179656 | tf_op jit(solution)/shard_map/ppermute | solution.py:17
  442.1 305.2 %all-reduce.2.cloned.1.call-start = ((), (), s32[]{:S(2)}) async-start(), calls=%async_computation.3 | async-start | bytes 131072 | tf_op jit(solution)/shard_map/psum | solution.py:213
  448.0 92.1 %collective-permute-start.9 = (bf16[3,16,8,512]{3,2,1,0:T(8,128)(2,1)S(1)}, bf16[3,16,8,512]{3,2,1,0:T(8,128)(2,1)}, u32[]{:S(2)}, u32[]{:S(2)}) collective-permute-start(bf16[3,16,8,512]{3,2,1,0:T(8,128)(2,1)S(1)} %collective-permute-done.8), channel_id=1, source_target_pairs={{1,0},{2,1},{3,2},{4,3},{5,4},{6,5},{7,6},{8,7},{9,8},{10,9},{11,1... | collective-permute-start | bytes 1179656 | tf_op jit(solution)/shard_map/ppermute | solution.py:17
  448.0 92.2 %collective-permute-start.26 = (bf16[3,16,8,512]{3,2,1,0:T(8,128)(2,1)S(1)}, bf16[3,16,8,512]{3,2,1,0:T(8,128)(2,1)}, u32[]{:S(2)}, u32[]{:S(2)}) collective-permute-start(bf16[3,16,8,512]{3,2,1,0:T(8,128)(2,1)S(1)} %broadcast_select_fusion.10), channel_id=1, source_target_pairs={{2,0},{3,1},{4,2},{5,3},{6,4},{7,5},{8,6},{9,7},{10,8},{11,9},{12,... | collective-permute-start | bytes 1179656 | tf_op jit(solution)/shard_map/ppermute | solution.py:17
  540.1 21.4 %collective-permute-start.10 = (bf16[3,16,8,512]{3,2,1,0:T(8,128)(2,1)S(1)}, bf16[3,16,8,512]{3,2,1,0:T(8,128)(2,1)S(1)}, u32[]{:S(2)}, u32[]{:S(2)}) collective-permute-start(bf16[3,16,8,512]{3,2,1,0:T(8,128)(2,1)S(1)} %broadcast_select_fusion.11), channel_id=1, source_target_pairs={{2,0},{3,1},{4,2},{5,3},{6,4},{7,5},{8,6},{9,7},{10,8},{11,9},{12,... | collective-permute-start | bytes 1179656 | tf_op jit(solution)/shard_map/ppermute | solution.py:17
  540.3 26.5 %collective-permute-start.27 = (bf16[3,16,8,512]{3,2,1,0:T(8,128)(2,1)S(1)}, bf16[3,16,8,512]{3,2,1,0:T(8,128)(2,1)S(1)}, u32[]{:S(2)}, u32[]{:S(2)}) collective-permute-start(bf16[3,16,8,512]{3,2,1,0:T(8,128)(2,1)S(1)} %broadcast_select_fusion.12), channel_id=1, source_target_pairs={{4,0},{5,1},{6,2},{7,3},{8,4},{9,5},{10,6},{11,7},{12,8},{13,9},{1... | collective-permute-start | bytes 1179656 | tf_op jit(solution)/shard_map/ppermute | solution.py:17
  561.5 40.6 %collective-permute-start.11 = (bf16[3,16,8,512]{3,2,1,0:T(8,128)(2,1)S(1)}, bf16[3,16,8,512]{3,2,1,0:T(8,128)(2,1)S(1)}, u32[]{:S(2)}, u32[]{:S(2)}) collective-permute-start(bf16[3,16,8,512]{3,2,1,0:T(8,128)(2,1)S(1)} %broadcast_select_fusion.13), channel_id=1, source_target_pairs={{4,0},{5,1},{6,2},{7,3},{8,4},{9,5},{10,6},{11,7},{12,8},{13,9},{1... | collective-permute-start | bytes 1179656 | tf_op jit(solution)/shard_map/ppermute | solution.py:17
  566.8 35.5 %collective-permute-start.28 = (bf16[3,16,8,512]{3,2,1,0:T(8,128)(2,1)S(1)}, bf16[3,16,8,512]{3,2,1,0:T(8,128)(2,1)S(1)}, u32[]{:S(2)}, u32[]{:S(2)}) collective-permute-start(bf16[3,16,8,512]{3,2,1,0:T(8,128)(2,1)S(1)} %broadcast_select_fusion.14), channel_id=1, source_target_pairs={{8,0},{9,1},{10,2},{11,3},{12,4},{13,5},{14,6},{15,7},{16,8},{17,9... | collective-permute-start | bytes 1179656 | tf_op jit(solution)/shard_map/ppermute | solution.py:17
  571.3 55.7 %collective-permute-start.31 = (bf16[11,7,8,512]{3,2,1,0:T(8,128)(2,1)S(1)}, bf16[11,7,8,512]{3,2,1,0:T(8,128)(2,1)S(1)}, u32[]{:S(2)}, u32[]{:S(2)}) collective-permute-start(bf16[11,7,8,512]{3,2,1,0:T(8,128)(2,1)S(1)} %pad_maximum_fusion.1), channel_id=1, source_target_pairs={{31,0},{0,1},{1,2},{2,3},{3,4},{4,5},{5,6},{6,7},{7,8},{8,9},{9,10... | collective-permute-start | bytes 1892360 | tf_op jit(solution)/shard_map/ppermute | solution.py:17
  571.4 76.5 %collective-permute-start.15 = (bf16[11,7,8,512]{3,2,1,0:T(8,128)(2,1)S(1)}, bf16[11,7,8,512]{3,2,1,0:T(8,128)(2,1)S(1)}, u32[]{:S(2)}, u32[]{:S(2)}) collective-permute-start(bf16[11,7,8,512]{3,2,1,0:T(8,128)(2,1)S(1)} %pad_maximum_fusion.2), channel_id=1, source_target_pairs={{31,0},{0,1},{1,2},{2,3},{3,4},{4,5},{5,6},{6,7},{7,8},{8,9},{9,10... | collective-permute-start | bytes 1892360 | tf_op jit(solution)/shard_map/ppermute | solution.py:17
  602.2 25.2 %collective-permute-start.12 = (bf16[3,16,8,512]{3,2,1,0:T(8,128)(2,1)S(1)}, bf16[3,16,8,512]{3,2,1,0:T(8,128)(2,1)S(1)}, u32[]{:S(2)}, u32[]{:S(2)}) collective-permute-start(bf16[3,16,8,512]{3,2,1,0:T(8,128)(2,1)S(1)} %broadcast_select_fusion.15), channel_id=1, source_target_pairs={{8,0},{9,1},{10,2},{11,3},{12,4},{13,5},{14,6},{15,7},{16,8},{17,9... | collective-permute-start | bytes 1179656 | tf_op jit(solution)/shard_map/ppermute | solution.py:17
  602.4 28.6 %collective-permute-start.29 = (bf16[3,16,8,512]{3,2,1,0:T(8,128)(2,1)S(1)}, bf16[3,16,8,512]{3,2,1,0:T(8,128)(2,1)S(1)}, u32[]{:S(2)}, u32[]{:S(2)}) collective-permute-start(bf16[3,16,8,512]{3,2,1,0:T(8,128)(2,1)S(1)} %broadcast_select_fusion.16), channel_id=1, source_target_pairs={{16,0},{17,1},{18,2},{19,3},{20,4},{21,5},{22,6},{23,7},{24,8},{25... | collective-permute-start | bytes 1179656 | tf_op jit(solution)/shard_map/ppermute | solution.py:17
  627.5 21.0 %collective-permute-start.13 = (bf16[3,16,8,512]{3,2,1,0:T(8,128)(2,1)S(1)}, bf16[3,16,8,512]{3,2,1,0:T(8,128)(2,1)S(1)}, u32[]{:S(2)}, u32[]{:S(2)}) collective-permute-start(bf16[3,16,8,512]{3,2,1,0:T(8,128)(2,1)S(1)} %broadcast_select_fusion.17), channel_id=1, source_target_pairs={{16,0},{17,1},{18,2},{19,3},{20,4},{21,5},{22,6},{23,7},{24,8},{25... | collective-permute-start | bytes 1179656 | tf_op jit(solution)/shard_map/ppermute | solution.py:17
  631.1 23.5 %collective-permute-start.30 = (bf16[3,16,8,512]{3,2,1,0:T(8,128)(2,1)S(1)}, bf16[3,16,8,512]{3,2,1,0:T(8,128)(2,1)S(1)}, u32[]{:S(2)}, u32[]{:S(2)}) collective-permute-start(bf16[3,16,8,512]{3,2,1,0:T(8,128)(2,1)S(1)} %broadcast_select_fusion.18), channel_id=1, source_target_pairs={{1,0},{2,1},{3,2},{4,3},{5,4},{6,5},{7,6},{8,7},{9,8},{10,9},{11,1... | collective-permute-start | bytes 1179656 | tf_op jit(solution)/shard_map/ppermute | solution.py:17
  (27 other events, 270.8 us)
Sparse Core Ops, SparseCore 0:
  58.9 71.1 all-gather.1
  442.3 115.6 reduce-scatter.1
  660.4 86.8 all-reduce.1
where the time goes:
time: 767 us; the launch traced here: 756 us
  waiting for transfers between devices  195 us (25%)
  blocking collectives  148 us (19%)
  starting transfers between devices  140 us (18%)
  local copies, waits for them, and re-layouts  114 us (15%)
  matrix products  69.8 us (9%)
  other arithmetic  63.6 us (8%)
  between operations  25.9 us (3%)
    ppermute x32, starting transfers between devices, shifted_2(): return lax.ppermute(block, axis, route)  140 us
    ppermute x32, waiting for transfers between devices, shifted_2(): return lax.ppermute(block, axis, route)  109 us
    psum x1, waiting for transfers between devices, on_device(): lax.psum(jnp.concatenate([term_qkv, term_out], axis=1).astype(jnp.bfloat1...  85.3 us
    psum x1, blocking collectives, on_device(): gain_total = lax.psum(jnp.sum(d_hidden * normed, axis=0), ('rad', 'azi'))  77.5 us
    all_gather x1, blocking collectives, on_device(): lax.all_gather(out_weight, 'azi', axis=0, tiled=True)  70.5 us
    another operation x4, local copies, waits for them, and re-layouts, to_windows(): tensor.reshape(extent_r // WR, WR, extent_a // WA, WA, extent_z // WZ, WZ...  38.5 us
    transpose x2, local copies, waits for them, and re-layouts, from_windows(): windows = windows.transpose(0, 5, 1, 6, 2, 7, 3, 4, 8)  27.3 us
    sub x1, other arithmetic, on_device(): weights = jax.nn.softmax(scores, axis=-1)  19.6 us
  transfers between devices with their start and end apart: 35, of which 12 were waited for; matrix products, arithmetic and copies ran while one was open for 6% of the time, Pallas kernels for 0%

commit v1 on v0

--- a/solution.py
+++ b/solution.py
@@ -9,6 +9,11 @@
 WA = 8
 WZ = 8
 EPS = 1e-05
+
+
+def gather_and_add(block, mesh_axis):
+    parts = lax.all_gather(block, mesh_axis)
+    return jnp.sum(parts, axis=0)
 
 
 def shifted_2(block, axis, distance):
@@ -212,7 +217,7 @@
     term_out = lax.dot_general(attended, grad_low, contract, preferred_element_type=jnp.float32)
     whole_term = lax.psum(jnp.concatenate([term_qkv, term_out], axis=1).astype(jnp.bfloat16), "rad")
     share = lax.psum_scatter(whole_term, "azi", scatter_dimension=0, tiled=True).astype(jnp.float32)
-    gain_total = lax.psum(jnp.sum(d_hidden * normed, axis=0), ("rad", "azi"))
+    gain_total = gather_and_add(jnp.sum(d_hidden * normed, axis=0), ("rad", "azi"))
     factor = float(number * n_rad * n_azi) ** (-0.5)
     grad_qkv = share[:, : 3 * width] * factor
     grad_out = share[:, 3 * width :] * factor

time: 767 us -> 1030 us (1.34)
  blocking collectives: 148 us -> 415 us
  starting transfers between devices: 140 us -> 77.2 us
  waiting for transfers between devices: 195 us -> 251 us
    all_gather x0 -> x1, blocking collectives: none -> 345 us  [gather_and_add(): parts = lax.all_gather(block, mesh_axis)]
    psum x1 -> x0, blocking collectives: 77.5 us -> none  [on_device(): gain_total = lax.psum(jnp.sum(d_hidden * normed, axis=0), ('rad', 'azi'))]
    ppermute x32, starting transfers between devices: 140 us -> 77.1 us  [shifted_2(): return lax.ppermute(block, axis, route)]
    ppermute x32, waiting for transfers between devices: 109 us -> 141 us  [shifted_2(): return lax.ppermute(block, axis, route)]
    psum x1, waiting for transfers between devices: 85.3 us -> 110 us  [on_device(): lax.psum(jnp.concatenate([term_qkv, term_out], axis=1).astype(jnp.bfloat1...]
  transfers between devices with their start and end apart: 35 -> 35, of which waited for: 12 -> 17; matrix products, arithmetic and copies ran while one was open for 6% -> 5% of each run, Pallas kernels for 0% -> 0%
where the time goes in v1:
time: 1030 us; the launch traced here: 1020 us
  blocking collectives  415 us (40%)
  waiting for transfers between devices  251 us (24%)
  local copies, waits for them, and re-layouts  114 us (11%)
  starting transfers between devices  77.2 us (7%)
  matrix products  69.8 us (7%)
  other arithmetic  65.7 us (6%)
  between operations  26 us (3%)
    all_gather x1, blocking collectives, gather_and_add(): parts = lax.all_gather(block, mesh_axis)  345 us
    ppermute x32, waiting for transfers between devices, shifted_2(): return lax.ppermute(block, axis, route)  141 us
    psum x1, waiting for transfers between devices, on_device(): lax.psum(jnp.concatenate([term_qkv, term_out], axis=1).astype(jnp.bfloat1...  110 us
    ppermute x32, starting transfers between devices, shifted_2(): return lax.ppermute(block, axis, route)  77.1 us
    all_gather x1, blocking collectives, on_device(): lax.all_gather(out_weight, 'azi', axis=0, tiled=True)  70.5 us
    another operation x4, local copies, waits for them, and re-layouts, to_windows(): tensor.reshape(extent_r // WR, WR, extent_a // WA, WA, extent_z // WZ, WZ...  38.5 us
    transpose x2, local copies, waits for them, and re-layouts, from_windows(): windows = windows.transpose(0, 5, 1, 6, 2, 7, 3, 4, 8)  27.3 us
  transfers between devices with their start and end apart: 35, of which 17 were waited for; matrix products, arithmetic and copies ran while one was open for 5% of the time, Pallas kernels for 0%

profile of v1, /device:TPU:32, one launch (start us, length us, event | category | flops | bytes accessed | tf_op | source)
XLA Modules:
  0.0 1019.5 jit_solution(1208263721121899287)
XLA Ops:
  32.1 8.7 collective-permute-start.19
  49.3 9.5 collective-permute-start.20
  60.8 10.2 %collective-permute-start.4 = (bf16[3,16,8,512]{3,2,1,0:T(8,128)(2,1)S(1)}, bf16[3,16,8,512]{3,2,1,0:T(8,128)(2,1)}, u32[]{:S(2)}, u32[]{:S(2)}) collective-permute-start(bf16[3,16,8,512]{3,2,1,0:T(8,128)(2,1)S(1)} %broadcast_select_fusion.3), channel_id=1, source_target_pairs={{4,0},{5,1},{6,2},{7,3},{8,4},{9,5},{10,6},{11,7},{12,8},{13,9},{1... | collective-permute-start | bytes 1179656 | tf_op jit(solution)/shard_map/ppermute | solution.py:22
  84.4 70.5 %all_gather.13 = bf16[512,512]{1,0:T(8,128)(2,1)} all-gather(bf16[16,512]{1,0:T(8,128)(2,1)S(1)} %copy-done.14), channel_id=1, replica_groups=mesh['rad'=8,'azi'=32] {'azi'}, dimensions={0}, use_global_device_ids=true | all-gather | bytes 540672 | tf_op jit(solution)/shard_map/all_gather | solution.py:159
  170.8 19.8 %collective-permute-done.5 = bf16[3,16,8,512]{3,2,1,0:T(8,128)(2,1)S(1)} collective-permute-done((bf16[3,16,8,512]{3,2,1,0:T(8,128)(2,1)S(1)}, bf16[3,16,8,512]{3,2,1,0:T(8,128)(2,1)S(1)}, u32[]{:S(2)}, u32[]{:S(2)}) %collective-permute-start.5) | collective-permute-done | bytes 393248 | tf_op jit(solution)/shard_map/ppermute | solution.py:22
  223.9 14.6 %reshape_reshape.12 = bf16[2,4,2,8,1,8,3,16,32]{8,7,6,5,3,2,1,0,4:T(8,128)(2,1)} reshape(bf16[1024,1536]{1,0:T(8,128)(2,1)} %convolution_convert_fusion) | data formatting | bytes 6291456 | tf_op jit(solution)/shard_map/reshape;reshape | solution.py:27
  238.5 12.8 %copy.37 = bf16[2,4,2,8,1,8,3,16,32]{8,5,3,1,7,6,2,0,4:T(8,128)(2,1)} copy(bf16[2,4,2,8,1,8,3,16,32]{8,7,6,5,3,2,1,0,4:T(8,128)(2,1)} %reshape_reshape.12) | data formatting | bytes 6291456 | tf_op jit(solution)/shard_map/reshape;reshape | solution.py:27
  251.2 11.6 %fusion.11 = f32[4,16,256,256]{2,3,1,0:T(8,128)} fusion(bf16[4,3,16,256,32]{4,3,2,1,0:T(8,128)(2,1)} %bitcast.106), kind=kOutput, calls=%fused_computation.19 | convolution fusion | flops 268435456 | bytes 25165824 | tf_op jit(solution)/shard_map/nhqd,nhkd->nhqk/dot_general | solution.py:166
  262.8 19.6 %fusion.62 = (f32[4,16,256]{2,1,0:T(8,128)S(1)}, f32[4,16,256,256]{2,3,1,0:T(8,128)}) fusion(f32[4,16,256,256]{2,3,1,0:T(8,128)} %fusion.11), kind=kOutput, calls=%fused_computation.143 | output fusion | flops 16777472 | bytes 33619968 | tf_op jit(solution)/shard_map/sub | solution.py:169
  282.4 14.5 %multiply_reduce_fusion = (f32[4,16,256]{2,1,0:T(8,128)S(1)}, f32[4,16,256,256]{2,3,1,0:T(8,128)}) fusion(f32[4,16,256,256]{2,3,1,0:T(8,128)} %get-tuple-element.18, f32[4,16,256]{2,1,0:T(8,128)S(1)} %get-tuple-element.17, bf16[4,16,256,32]{3,2,1,0:T(8,128)(2,1)} %bitcast.121, bf16[4,3,16,256,32]{4,3,2,1,0:T(8,128)(2,1)} %bitcast.107), kind=kOutput, calls=%fused_computation.2 | convolution fusion | flops 281001984 | bytes 42074112 | tf_op jit(solution)/shard_map/nhqd,nhkd->nhqk/dot_general | solution.py:181
  296.9 11.7 %multiply_convert_fusion = bf16[4,16,256,256]{2,3,1,0:T(8,128)(2,1)S(1)} fusion(f32[4,16,256,256]{2,3,1,0:T(8,128)} %get-tuple-element.20, f32[4,16,256]{2,1,0:T(8,128)S(1)} %get-tuple-element.19, f32[4,16,256,256]{2,3,1,0:T(8,128)} %get-tuple-element.18, f32[4,16,256]{2,1,0:T(8,128)S(1)} %get-tuple-element.17), kind=kLoop, calls=%fused_computation.1 | loop fusion | flops 16777216 | bytes 42074112 | tf_op jit(solution)/shard_map/convert_element_type | solution.py:187
  322.7 9.3 fusion.34
  332.0 9.7 fusion.31
  357.1 16.4 %copy.53 = bf16[2,4,2,8,1,8,3,16,32]{8,7,6,5,3,2,1,0,4:T(8,128)(2,1)} copy(bf16[2,4,2,8,1,8,3,16,32]{8,5,3,1,7,2,0,6,4:T(8,128)(2,1)S(1)} %maximum_bitcast_fusion) | data formatting | bytes 6291456 | tf_op jit(solution)/shard_map/transpose | solution.py:39
  373.5 17.1 %reshape_reshape.15 = bf16[1024,1536]{1,0:T(8,128)(2,1)} reshape(bf16[2,4,2,8,1,8,3,16,32]{8,7,6,5,3,2,1,0,4:T(8,128)(2,1)} %copy.53) | data formatting | bytes 6291456 | tf_op jit(solution)/shard_map/reshape;reshape | solution.py:197
  393.6 10.8 %copy.43 = bf16[2,4,2,8,1,8,1,16,32]{8,7,5,3,2,1,0,6,4:T(8,128)(2,1)} copy(bf16[2,4,2,8,1,8,1,16,32]{8,5,3,1,7,2,0,6,4:T(8,128)(2,1)} %bitcast.111) | data formatting | bytes 2097152 | tf_op jit(solution)/shard_map/transpose | solution.py:39
  421.1 12.5 %collective-permute-done.24 = bf16[3,16,8,512]{3,2,1,0:T(8,128)(2,1)S(1)} collective-permute-done((bf16[3,16,8,512]{3,2,1,0:T(8,128)(2,1)S(1)}, bf16[3,16,8,512]{3,2,1,0:T(8,128)(2,1)S(1)}, u32[]{:S(2)}, u32[]{:S(2)}) %collective-permute-start.24) | collective-permute-done | bytes 393248 | tf_op jit(solution)/shard_map/ppermute | solution.py:22
  442.5 12.7 %collective-permute-start.26 = (bf16[3,16,8,512]{3,2,1,0:T(8,128)(2,1)}, bf16[3,16,8,512]{3,2,1,0:T(8,128)(2,1)}, u32[]{:S(2)}, u32[]{:S(2)}) collective-permute-start(bf16[3,16,8,512]{3,2,1,0:T(8,128)(2,1)} %broadcast_select_fusion.10), channel_id=1, source_target_pairs={{2,0},{3,1},{4,2},{5,3},{6,4},{7,5},{8,6},{9,7},{10,8},{11,9},{12,... | collective-permute-start | bytes 1179656 | tf_op jit(solution)/shard_map/ppermute | solution.py:22
  455.2 344.7 %all-gather.1 = f32[256,1,512]{2,1,0:T(1,128)S(1)} all-gather(f32[1,1,512]{2,1,0:T(1,128)S(1)} %bitcast.125), channel_id=2, replica_groups=mesh['rad'=8,'azi'=32] {'rad','azi'}, dimensions={0}, use_global_device_ids=true | all-gather | bytes 526336 | tf_op jit(solution)/shard_map/all_gather | solution.py:15
  810.1 15.8 %collective-permute-done.10 = bf16[3,16,8,512]{3,2,1,0:T(8,128)(2,1)S(1)} collective-permute-done((bf16[3,16,8,512]{3,2,1,0:T(8,128)(2,1)S(1)}, bf16[3,16,8,512]{3,2,1,0:T(8,128)(2,1)S(1)}, u32[]{:S(2)}, u32[]{:S(2)}) %collective-permute-start.10) | collective-permute-done | bytes 393248 | tf_op jit(solution)/shard_map/ppermute | solution.py:22
  826.1 14.2 %collective-permute-done.27 = bf16[3,16,8,512]{3,2,1,0:T(8,128)(2,1)S(1)} collective-permute-done((bf16[3,16,8,512]{3,2,1,0:T(8,128)(2,1)S(1)}, bf16[3,16,8,512]{3,2,1,0:T(8,128)(2,1)S(1)}, u32[]{:S(2)}, u32[]{:S(2)}) %collective-permute-start.27) | collective-permute-done | bytes 393248 | tf_op jit(solution)/shard_map/ppermute | solution.py:22
  840.7 19.5 %collective-permute-done.11 = bf16[3,16,8,512]{3,2,1,0:T(8,128)(2,1)S(1)} collective-permute-done((bf16[3,16,8,512]{3,2,1,0:T(8,128)(2,1)S(1)}, bf16[3,16,8,512]{3,2,1,0:T(8,128)(2,1)S(1)}, u32[]{:S(2)}, u32[]{:S(2)}) %collective-permute-start.11) | collective-permute-done | bytes 393248 | tf_op jit(solution)/shard_map/ppermute | solution.py:22
  860.3 9.4 collective-permute-done.28
  900.6 109.8 %all-reduce.2.cloned.1.call-done = bf16[16,2048]{1,0:T(8,128)(2,1)} async-done(((bf16[16,2048]{1,0:T(8,128)(2,1)}), bf16[16,2048]{1,0:T(8,128)(2,1)}) %all-reduce.2.cloned.1.call-update) | async-done | bytes 65552 | tf_op jit(solution)/shard_map/psum | solution.py:218
  (176 shorter events, 188.4 us)
Async XLA Ops:
  7.2 211.9 %all-gather.4.cloned.1.call-start = ((), (), s32[]{:S(2)}) async-start(), calls=%async_computation.1 | async-start | bytes 1622016 | tf_op jit(solution)/shard_map/all_gather | solution.py:158
  14.9 15.8 %collective-permute-start = (bf16[3,16,8,512]{3,2,1,0:T(8,128)(2,1)S(1)}, bf16[3,16,8,512]{3,2,1,0:T(8,128)(2,1)S(1)}, u32[]{:S(2)}, u32[]{:S(2)}) collective-permute-start(bf16[3,16,8,512]{3,2,1,0:T(8,128)(2,1)S(1)} %slice.79), channel_id=1, source_target_pairs={{32,0},{64,32},{96,64},{128,96},{160,128},{192,160},{224,192},{0,2... | collective-permute-start | bytes 1179656 | tf_op jit(solution)/shard_map/ppermute | solution.py:22
  32.1 16.4 %collective-permute-start.19 = (bf16[3,16,8,512]{3,2,1,0:T(8,128)(2,1)S(1)}, bf16[3,16,8,512]{3,2,1,0:T(8,128)(2,1)S(1)}, u32[]{:S(2)}, u32[]{:S(2)}) collective-permute-start(bf16[3,16,8,512]{3,2,1,0:T(8,128)(2,1)S(1)} %get-tuple-element.10), channel_id=1, source_target_pairs={{2,0},{3,1},{4,2},{5,3},{6,4},{7,5},{8,6},{9,7},{10,8},{11,9},{12,... | collective-permute-start | bytes 1179656 | tf_op jit(solution)/shard_map/ppermute | solution.py:22
  43.3 16.5 %collective-permute-start.3 = (bf16[3,16,8,512]{3,2,1,0:T(8,128)(2,1)S(1)}, bf16[3,16,8,512]{3,2,1,0:T(8,128)(2,1)}, u32[]{:S(2)}, u32[]{:S(2)}) collective-permute-start(bf16[3,16,8,512]{3,2,1,0:T(8,128)(2,1)S(1)} %get-tuple-element.12), channel_id=1, source_target_pairs={{2,0},{3,1},{4,2},{5,3},{6,4},{7,5},{8,6},{9,7},{10,8},{11,9},{12,... | collective-permute-start | bytes 1179656 | tf_op jit(solution)/shard_map/ppermute | solution.py:22
  49.3 29.0 %collective-permute-start.20 = (bf16[3,16,8,512]{3,2,1,0:T(8,128)(2,1)}, bf16[3,16,8,512]{3,2,1,0:T(8,128)(2,1)}, u32[]{:S(2)}, u32[]{:S(2)}) collective-permute-start(bf16[3,16,8,512]{3,2,1,0:T(8,128)(2,1)} %broadcast_select_fusion.2), channel_id=1, source_target_pairs={{4,0},{5,1},{6,2},{7,3},{8,4},{9,5},{10,6},{11,7},{12,8},{13,9},{1... | collective-permute-start | bytes 1179656 | tf_op jit(solution)/shard_map/ppermute | solution.py:22
  58.8 840.0 %reduce-scatter.2.cloned.1.call-start = ((), (), s32[]{:S(2)}) async-start(), calls=%async_computation.2 | async-start | bytes 2162688 | tf_op jit(solution)/shard_map/reduce_scatter | solution.py:219
  59.8 109.5 %collective-permute-start.17 = (bf16[11,7,8,512]{3,2,1,0:T(8,128)(2,1)}, bf16[11,7,8,512]{3,2,1,0:T(8,128)(2,1)}, u32[]{:S(2)}, u32[]{:S(2)}) collective-permute-start(bf16[11,7,8,512]{3,2,1,0:T(8,128)(2,1)} %slice.113), channel_id=1, source_target_pairs={{1,0},{2,1},{3,2},{4,3},{5,4},{6,5},{7,6},{8,7},{9,8},{10,9},{11,1... | collective-permute-start | bytes 1892360 | tf_op jit(solution)/shard_map/ppermute | solution.py:22
  60.8 104.0 %collective-permute-start.4 = (bf16[3,16,8,512]{3,2,1,0:T(8,128)(2,1)S(1)}, bf16[3,16,8,512]{3,2,1,0:T(8,128)(2,1)}, u32[]{:S(2)}, u32[]{:S(2)}) collective-permute-start(bf16[3,16,8,512]{3,2,1,0:T(8,128)(2,1)S(1)} %broadcast_select_fusion.3), channel_id=1, source_target_pairs={{4,0},{5,1},{6,2},{7,3},{8,4},{9,5},{10,6},{11,7},{12,8},{13,9},{1... | collective-permute-start | bytes 1179656 | tf_op jit(solution)/shard_map/ppermute | solution.py:22
  80.1 86.5 %collective-permute-start.21 = (bf16[3,16,8,512]{3,2,1,0:T(8,128)(2,1)}, bf16[3,16,8,512]{3,2,1,0:T(8,128)(2,1)}, u32[]{:S(2)}, u32[]{:S(2)}) collective-permute-start(bf16[3,16,8,512]{3,2,1,0:T(8,128)(2,1)} %broadcast_select_fusion.4), channel_id=1, source_target_pairs={{8,0},{9,1},{10,2},{11,3},{12,4},{13,5},{14,6},{15,7},{16,8},{17,9... | collective-permute-start | bytes 1179656 | tf_op jit(solution)/shard_map/ppermute | solution.py:22
  164.8 26.8 %collective-permute-start.1 = (bf16[11,7,8,512]{3,2,1,0:T(8,128)(2,1)S(1)}, bf16[11,7,8,512]{3,2,1,0:T(8,128)(2,1)S(1)}, u32[]{:S(2)}, u32[]{:S(2)}) collective-permute-start(bf16[11,7,8,512]{3,2,1,0:T(8,128)(2,1)S(1)} %slice.104), channel_id=1, source_target_pairs={{1,0},{2,1},{3,2},{4,3},{5,4},{6,5},{7,6},{8,7},{9,8},{10,9},{11,1... | collective-permute-start | bytes 1892360 | tf_op jit(solution)/shard_map/ppermute | solution.py:22
  165.9 24.8 %collective-permute-start.5 = (bf16[3,16,8,512]{3,2,1,0:T(8,128)(2,1)S(1)}, bf16[3,16,8,512]{3,2,1,0:T(8,128)(2,1)S(1)}, u32[]{:S(2)}, u32[]{:S(2)}) collective-permute-start(bf16[3,16,8,512]{3,2,1,0:T(8,128)(2,1)S(1)} %broadcast_select_fusion.5), channel_id=1, source_target_pairs={{8,0},{9,1},{10,2},{11,3},{12,4},{13,5},{14,6},{15,7},{16,8},{17,9... | collective-permute-start | bytes 1179656 | tf_op jit(solution)/shard_map/ppermute | solution.py:22
  167.6 23.8 %collective-permute-start.22 = (bf16[3,16,8,512]{3,2,1,0:T(8,128)(2,1)S(1)}, bf16[3,16,8,512]{3,2,1,0:T(8,128)(2,1)S(1)}, u32[]{:S(2)}, u32[]{:S(2)}) collective-permute-start(bf16[3,16,8,512]{3,2,1,0:T(8,128)(2,1)S(1)} %broadcast_select_fusion.6), channel_id=1, source_target_pairs={{16,0},{17,1},{18,2},{19,3},{20,4},{21,5},{22,6},{23,7},{24,8},{25... | collective-permute-start | bytes 1179656 | tf_op jit(solution)/shard_map/ppermute | solution.py:22
  416.9 16.7 %collective-permute-start.24 = (bf16[3,16,8,512]{3,2,1,0:T(8,128)(2,1)S(1)}, bf16[3,16,8,512]{3,2,1,0:T(8,128)(2,1)S(1)}, u32[]{:S(2)}, u32[]{:S(2)}) collective-permute-start(bf16[3,16,8,512]{3,2,1,0:T(8,128)(2,1)S(1)} %bitcast.124), channel_id=1, source_target_pairs={{224,0},{0,32},{32,64},{64,96},{96,128},{128,160},{160,192},{192,2... | collective-permute-start | bytes 1179656 | tf_op jit(solution)/shard_map/ppermute | solution.py:22
  418.6 23.1 %collective-permute-start.8 = (bf16[3,16,8,512]{3,2,1,0:T(8,128)(2,1)}, bf16[3,16,8,512]{3,2,1,0:T(8,128)(2,1)S(1)}, u32[]{:S(2)}, u32[]{:S(2)}) collective-permute-start(bf16[3,16,8,512]{3,2,1,0:T(8,128)(2,1)} %bitcast.13), channel_id=1, source_target_pairs={{224,0},{0,32},{32,64},{64,96},{96,128},{128,160},{160,192},{192,2... | collective-permute-start | bytes 1179656 | tf_op jit(solution)/shard_map/ppermute | solution.py:22
  436.0 574.4 %all-reduce.2.cloned.1.call-start = ((), (), s32[]{:S(2)}) async-start(), calls=%async_computation.3 | async-start | bytes 131072 | tf_op jit(solution)/shard_map/psum | solution.py:218
  441.7 358.5 %collective-permute-start.9 = (bf16[3,16,8,512]{3,2,1,0:T(8,128)(2,1)S(1)}, bf16[3,16,8,512]{3,2,1,0:T(8,128)(2,1)}, u32[]{:S(2)}, u32[]{:S(2)}) collective-permute-start(bf16[3,16,8,512]{3,2,1,0:T(8,128)(2,1)S(1)} %collective-permute-done.8), channel_id=1, source_target_pairs={{1,0},{2,1},{3,2},{4,3},{5,4},{6,5},{7,6},{8,7},{9,8},{10,9},{11,1... | collective-permute-start | bytes 1179656 | tf_op jit(solution)/shard_map/ppermute | solution.py:22
  442.5 365.9 %collective-permute-start.26 = (bf16[3,16,8,512]{3,2,1,0:T(8,128)(2,1)}, bf16[3,16,8,512]{3,2,1,0:T(8,128)(2,1)}, u32[]{:S(2)}, u32[]{:S(2)}) collective-permute-start(bf16[3,16,8,512]{3,2,1,0:T(8,128)(2,1)} %broadcast_select_fusion.10), channel_id=1, source_target_pairs={{2,0},{3,1},{4,2},{5,3},{6,4},{7,5},{8,6},{9,7},{10,8},{11,9},{12,... | collective-permute-start | bytes 1179656 | tf_op jit(solution)/shard_map/ppermute | solution.py:22
  800.3 25.6 %collective-permute-start.10 = (bf16[3,16,8,512]{3,2,1,0:T(8,128)(2,1)S(1)}, bf16[3,16,8,512]{3,2,1,0:T(8,128)(2,1)S(1)}, u32[]{:S(2)}, u32[]{:S(2)}) collective-permute-start(bf16[3,16,8,512]{3,2,1,0:T(8,128)(2,1)S(1)} %broadcast_select_fusion.11), channel_id=1, source_target_pairs={{2,0},{3,1},{4,2},{5,3},{6,4},{7,5},{8,6},{9,7},{10,8},{11,9},{12,... | collective-permute-start | bytes 1179656 | tf_op jit(solution)/shard_map/ppermute | solution.py:22
  809.5 30.7 %collective-permute-start.27 = (bf16[3,16,8,512]{3,2,1,0:T(8,128)(2,1)S(1)}, bf16[3,16,8,512]{3,2,1,0:T(8,128)(2,1)S(1)}, u32[]{:S(2)}, u32[]{:S(2)}) collective-permute-start(bf16[3,16,8,512]{3,2,1,0:T(8,128)(2,1)S(1)} %broadcast_select_fusion.12), channel_id=1, source_target_pairs={{4,0},{5,1},{6,2},{7,3},{8,4},{9,5},{10,6},{11,7},{12,8},{13,9},{1... | collective-permute-start | bytes 1179656 | tf_op jit(solution)/shard_map/ppermute | solution.py:22
  826.0 34.2 %collective-permute-start.11 = (bf16[3,16,8,512]{3,2,1,0:T(8,128)(2,1)S(1)}, bf16[3,16,8,512]{3,2,1,0:T(8,128)(2,1)S(1)}, u32[]{:S(2)}, u32[]{:S(2)}) collective-permute-start(bf16[3,16,8,512]{3,2,1,0:T(8,128)(2,1)S(1)} %broadcast_select_fusion.13), channel_id=1, source_target_pairs={{4,0},{5,1},{6,2},{7,3},{8,4},{9,5},{10,6},{11,7},{12,8},{13,9},{1... | collective-permute-start | bytes 1179656 | tf_op jit(solution)/shard_map/ppermute | solution.py:22
  840.3 29.5 %collective-permute-start.28 = (bf16[3,16,8,512]{3,2,1,0:T(8,128)(2,1)S(1)}, bf16[3,16,8,512]{3,2,1,0:T(8,128)(2,1)S(1)}, u32[]{:S(2)}, u32[]{:S(2)}) collective-permute-start(bf16[3,16,8,512]{3,2,1,0:T(8,128)(2,1)S(1)} %broadcast_select_fusion.14), channel_id=1, source_target_pairs={{8,0},{9,1},{10,2},{11,3},{12,4},{13,5},{14,6},{15,7},{16,8},{17,9... | collective-permute-start | bytes 1179656 | tf_op jit(solution)/shard_map/ppermute | solution.py:22
  840.4 29.5 %collective-permute-start.31 = (bf16[11,7,8,512]{3,2,1,0:T(8,128)(2,1)S(1)}, bf16[11,7,8,512]{3,2,1,0:T(8,128)(2,1)S(1)}, u32[]{:S(2)}, u32[]{:S(2)}) collective-permute-start(bf16[11,7,8,512]{3,2,1,0:T(8,128)(2,1)S(1)} %pad_maximum_fusion.1), channel_id=1, source_target_pairs={{31,0},{0,1},{1,2},{2,3},{3,4},{4,5},{5,6},{6,7},{7,8},{8,9},{9,10... | collective-permute-start | bytes 1892360 | tf_op jit(solution)/shard_map/ppermute | solution.py:22
  840.6 44.8 %collective-permute-start.15 = (bf16[11,7,8,512]{3,2,1,0:T(8,128)(2,1)S(1)}, bf16[11,7,8,512]{3,2,1,0:T(8,128)(2,1)S(1)}, u32[]{:S(2)}, u32[]{:S(2)}) collective-permute-start(bf16[11,7,8,512]{3,2,1,0:T(8,128)(2,1)S(1)} %pad_maximum_fusion.2), channel_id=1, source_target_pairs={{31,0},{0,1},{1,2},{2,3},{3,4},{4,5},{5,6},{6,7},{7,8},{8,9},{9,10... | collective-permute-start | bytes 1892360 | tf_op jit(solution)/shard_map/ppermute | solution.py:22
  860.2 17.9 %collective-permute-start.12 = (bf16[3,16,8,512]{3,2,1,0:T(8,128)(2,1)S(1)}, bf16[3,16,8,512]{3,2,1,0:T(8,128)(2,1)S(1)}, u32[]{:S(2)}, u32[]{:S(2)}) collective-permute-start(bf16[3,16,8,512]{3,2,1,0:T(8,128)(2,1)S(1)} %broadcast_select_fusion.15), channel_id=1, source_target_pairs={{8,0},{9,1},{10,2},{11,3},{12,4},{13,5},{14,6},{15,7},{16,8},{17,9... | collective-permute-start | bytes 1179656 | tf_op jit(solution)/shard_map/ppermute | solution.py:22
  (27 other events, 246.7 us)
Sparse Core Ops, SparseCore 0:
  58.9 71.1 all-gather.3
  436.1 117.9 reduce-scatter.1
  899.0 111.2 all-reduce.1
